TPU v7x, 32 devices: a whole 2x2x4 slice. The times are simulated.
32 devices in a mesh: ex: 2 (over core), ey: 16 (over z, y, x).
Axes of the slice: x: 2, y: 2, z: 4, core: 2. Of those that a mesh axis runs over, the one named last changes fastest.
Arguments:
- tokens: bfloat16 [32, 256, 1024], P(('ex', 'ey')), may hold values from -16 to 16
- slot_param: bfloat16 [1024, 32], replicated, may hold values from -0.75 to 0.75
- weight_in: bfloat16 [32, 1024, 4096], P('ey', None, 'ex'), may hold values from -0.1875 to 0.1875
- weight_out: bfloat16 [32, 4096, 1024], P('ey', 'ex'), may hold values from -0.09375 to 0.09375
- grad_out: bfloat16 [32, 256, 1024], P(('ex', 'ey')), may hold values from -6 to 6
Outputs:
- grad_tokens: bfloat16 [32, 256, 1024], P(('ex', 'ey'))
- grad_param: float32 [1024, 32], replicated
- grad_win: bfloat16 [32, 1024, 4096], P('ey', None, 'ex')
- grad_wout: bfloat16 [32, 4096, 1024], P('ey', 'ex')
All inputs are finite; a program needn't handle non-finite values.
Results may differ from a plain program's by a relative error of at most 0.017.
Values may be sent and summed in bfloat16 or wider, within the bound.
No kernel may reach another device: no remote copies, remote signals or barrier semaphores. Data moves between devices by JAX's collectives and lax.ppermute only.
A program may use at most 64 MiB of HBM per device.

v0:
```python
import jax
import jax.numpy as jnp
from jax import lax
from jax.sharding import PartitionSpec as P


def gelu_parts(pre):
    cdf = 0.5 * (1.0 + lax.erf(pre * 0.7071067811865476))
    slope = cdf + pre * jnp.exp(-0.5 * pre * pre) * 0.3989422804014327
    return (pre * cdf, slope)


def softmax_along(values, axis):
    top = jnp.max(values, axis=axis, keepdims=True)
    expo = jnp.exp(values - top)
    return expo / jnp.sum(expo, axis=axis, keepdims=True)


def route_in(stacked):
    moved = lax.all_to_all(stacked, "ey", split_axis=2, concat_axis=0, tiled=True)
    return lax.all_gather(moved, "ex", axis=0, tiled=True)


def route_out(term_fn, total_rows):
    summed = lax.psum_scatter(
        term_fn(jnp.int32(0), total_rows // lax.axis_size("ex") * lax.axis_size("ex")).astype(
            jnp.bfloat16
        ),
        "ex",
        scatter_dimension=0,
        tiled=True,
    )
    return lax.all_to_all(summed, "ey", split_axis=0, concat_axis=2, tiled=True)


def per_device(tokens, slot_param, weight_in, weight_out, grad_out):
    logits = jnp.einsum("ipd,ds->ips", tokens, slot_param, preferred_element_type=jnp.float32)
    dispatch = softmax_along(logits, 1)
    combine = softmax_along(logits, 2)
    dispatch_b = dispatch.astype(jnp.bfloat16)
    combine_b = combine.astype(jnp.bfloat16)
    slot_in = jnp.einsum(
        "ips,ipd->isd", dispatch_b, tokens, preferred_element_type=jnp.float32
    ).astype(jnp.bfloat16)
    slot_cot = jnp.einsum(
        "ips,ipd->isd", combine_b, grad_out, preferred_element_type=jnp.float32
    ).astype(jnp.bfloat16)
    arrived = route_in(jnp.stack((slot_in, slot_cot), axis=1))
    total_rows = arrived.shape[0]
    slot_x = arrived[:, 0]
    slot_g = arrived[:, 1]
    pre = jnp.einsum("red,edf->ref", slot_x, weight_in, preferred_element_type=jnp.float32)
    value, slope = gelu_parts(pre)
    hidden = value.astype(jnp.bfloat16)
    back = jnp.einsum("red,efd->ref", slot_g, weight_out, preferred_element_type=jnp.float32)
    dpre = (back * slope).astype(jnp.bfloat16)

    def paired_term(start, count):
        return jnp.concatenate(
            (
                jnp.einsum("ref,efd->red", hidden, weight_out, preferred_element_type=jnp.float32)[
                    :, None
                ],
                jnp.einsum("ref,edf->red", dpre, weight_in, preferred_element_type=jnp.float32)[
                    :, None
                ],
            ),
            axis=1,
        )

    paired = route_out(paired_term, total_rows)
    slot_out = paired[:, 0]
    grad_slot = paired[:, 1]
    grad_win = jnp.einsum("red,ref->edf", slot_x, dpre, preferred_element_type=jnp.float32).astype(
        jnp.bfloat16
    )
    grad_wout = jnp.einsum(
        "ref,red->efd", hidden, slot_g, preferred_element_type=jnp.float32
    ).astype(jnp.bfloat16)
    d_combine = jnp.einsum("ipd,isd->ips", grad_out, slot_out, preferred_element_type=jnp.float32)
    d_dispatch = jnp.einsum("ipd,isd->ips", tokens, grad_slot, preferred_element_type=jnp.float32)
    d_logits = dispatch * (d_dispatch - jnp.sum(dispatch * d_dispatch, axis=1, keepdims=True))
    d_logits = d_logits + combine * (
        d_combine - jnp.sum(combine * d_combine, axis=2, keepdims=True)
    )
    logit_grad = d_logits.astype(jnp.bfloat16)
    grad_tokens = jnp.einsum(
        "ips,isd->ipd", dispatch_b, grad_slot, preferred_element_type=jnp.float32
    )
    grad_tokens = grad_tokens + jnp.einsum(
        "ips,ds->ipd", logit_grad, slot_param, preferred_element_type=jnp.float32
    )
    local_param = jnp.einsum("ipd,ips->ds", tokens, logit_grad, preferred_element_type=jnp.float32)
    grad_param = lax.psum(local_param, ("ex", "ey"))
    return (grad_tokens.astype(jnp.bfloat16), grad_param, grad_win, grad_wout)


def solution(mesh):
    in_specs = (
        P(("ex", "ey"), None, None),
        P(),
        P("ey", None, "ex"),
        P("ey", "ex", None),
        P(("ex", "ey"), None, None),
    )
    out_specs = (P(("ex", "ey"), None, None), P(), P("ey", None, "ex"), P("ey", "ex", None))
    return jax.shard_map(
        per_device, mesh=mesh, in_specs=in_specs, out_specs=out_specs, check_vma=False
    )
```

profile of v0, /device:TPU:0, one launch (start us, length us, event | category | flops | bytes accessed | tf_op | source)
XLA Modules:
  0.0 198.2 jit_solution(10697608207090606354)
XLA Ops:
  7.2 1.0 copy-done
  8.2 1.2 fusion.36
  9.6 0.2 fusion.6
  9.9 1.2 fusion.7
  11.3 15.9 %all_to_all.36 = bf16[1,2,32,1024]{3,1,0,2:T(2,128)(2,1)S(1)} all-to-all(bf16[1,2,32,1024]{3,1,0,2:T(2,128)(2,1)S(1)} %copy.17), channel_id=1, replica_groups=mesh['ex'=2,'ey'=16] {'ey'}, dimensions={2} | all-to-all | bytes 262144 | tf_op jit(solution)/shard_map/all_to_all | solution.py:20
  27.3 2.1 %all-gather = bf16[32,1,2,2,1024]{4,0,3,2,1:T(8,128)(2,1)S(1)} all-gather(bf16[16,1,2,2,1024]{4,0,3,2,1:T(8,128)(2,1)S(1)} %bitcast.90), channel_id=2, replica_groups=mesh['ex'=2,'ey'=16] {'ex'}, dimensions={0}, use_global_device_ids=true | all-gather | bytes 393216 | tf_op jit(solution)/shard_map/all_gather | solution.py:21
  29.4 5.1 %convolution_bitcast_fusion.1 = f32[32,2,2048]{2,0,1:T(8,128)S(1)} fusion(bf16[2,1024,2048]{2,1,0:T(8,128)(2,1)} %param.7, bf16[32,2,2,1024]{3,0,2,1:T(8,128)(2,1)S(1)} %bitcast.85), kind=kOutput, calls=%fused_computation.4 | convolution fusion | flops 268435456 | bytes 9043968 | tf_op jit(solution)/shard_map/red,edf->ref/dot_general | solution.py:52
  34.5 1.5 fusion.4
  36.0 2.6 %fusion.1 = bf16[32,2,2048]{2,0,1:T(8,128)(2,1)S(1)} fusion(bf16[2,2048,1024]{2,1,0:T(8,128)(2,1)S(1)} %bitcast.82, f32[32,2,2048]{2,0,1:T(8,128)S(1)} %convolution_bitcast_fusion.1, bf16[32,2,2,1024]{3,0,2,1:T(8,128)(2,1)S(1)} %bitcast.86), kind=kOutput, calls=%fused_computation.5 | convolution fusion | flops 269746176 | bytes 9306112 | tf_op jit(solution)/shard_map/red,efd->ref/dot_general | solution.py:55
  38.7 2.6 %fusion.5 = bf16[32,1,2,1024]{3,0,2,1:T(8,128)(2,1)S(1)} fusion(bf16[32,2,2048]{2,0,1:T(8,128)(2,1)S(1)} %fusion.1, bf16[2,1024,2048]{2,1,0:T(8,128)(2,1)S(1)} %bitcast.84), kind=kOutput, calls=%fused_computation.12 | convolution fusion | flops 268500992 | bytes 8781824 | tf_op jit(solution)/shard_map/ref,edf->red/dot_general | solution.py:64
  41.2 0.7 pad_maximum_fusion
  42.0 5.8 %convolution_convert_fusion = bf16[2,2048,1024]{2,1,0:T(8,128)(2,1)} fusion(bf16[32,2,2,1024]{3,0,2,1:T(8,128)(2,1)S(1)} %bitcast.87, f32[32,2,2048]{2,0,1:T(8,128)S(1)} %convolution_bitcast_fusion.1), kind=kOutput, calls=%fused_computation | convolution fusion | flops 273285120 | bytes 9043968 | tf_op jit(solution)/shard_map/ref,red->efd/dot_general | solution.py:77
  47.8 1.7 copy.19
  49.5 6.0 %all-to-all-start.1 = ((bf16[16,2,2,1024]{3,2,1,0:T(2,128)(2,1)}), bf16[16,2,2,1024]{3,2,1,0:T(2,128)(2,1)S(1)}, u32[]{:S(2)}, u32[]{:S(2)}) async-start(bf16[16,2,2,1024]{3,2,1,0:T(2,128)(2,1)} %copy.19), calls=%async_computation.2 | async-start | bytes 262144 | tf_op jit(solution)/shard_map/all_to_all | solution.py:33
  55.5 0.2 all-reduce.2.cloned.1.call-start
  55.8 5.8 %convolution_convert_fusion.1 = bf16[2,1024,2048]{2,1,0:T(8,128)(2,1)} fusion(bf16[32,2,2048]{2,0,1:T(8,128)(2,1)S(1)} %fusion.1, bf16[32,2,2,1024]{3,0,2,1:T(8,128)(2,1)S(1)} %bitcast.88), kind=kOutput, calls=%fused_computation.1 | convolution fusion | flops 272629760 | bytes 8781824 | tf_op jit(solution)/shard_map/red,ref->edf/dot_general | solution.py:74
  61.6 1.9 all-to-all-done.1
  63.8 0.3 convolution_bitcast_fusion.3
  64.1 0.4 fusion.22
  64.5 0.4 multiply_reduce_fusion.1
  64.8 0.9 convolution_bitcast_fusion.2
  65.8 1.2 fusion.3
  67.0 122.8 %all-reduce.2.cloned.1.call-done = f32[1024,32]{0,1:T(8,128)} async-done(((f32[1024,32]{0,1:T(8,128)}), f32[1024,32]{0,1:T(8,128)}) %all-reduce.2.cloned.1.call-update) | async-done | bytes 131088 | tf_op jit(solution)/shard_map/psum | solution.py:94
  189.8 1.6 copy.40
  (25 shorter events, 0.8 us)
Async XLA Ops:
  7.2 1.0 copy-start
  7.2 40.6 %reduce-scatter.2.cloned.1.call-start = ((), (), s32[]{:S(2)}) async-start(), calls=%async_computation.3 | async-start | bytes 393216 | tf_op jit(solution)/shard_map/reduce_scatter | solution.py:25
  27.2 7.3 %slice-start = ((s8[8388608]{0:T(1024)(128)(4,1)}), s8[4194304]{0:T(1024)(128)(4,1)S(1)}, s32[]{:S(2)}) async-start(s8[8388608]{0:T(1024)(128)(4,1)} %bitcast.81), calls=%async_computation.5 | async-start | bytes 8388608
  29.4 5.1 %slice-start.1 = ((s8[8388608]{0:T(1024)(128)(4,1)}), s8[4194304]{0:T(1024)(128)(4,1)S(1)}, s32[]{:S(2)}) async-start(s8[8388608]{0:T(1024)(128)(4,1)} %bitcast.81), calls=%async_computation.6 | async-start | bytes 8388608
  29.4 9.3 %slice-start.2 = ((s8[8388608]{0:T(1024)(128)(4,1)}), s8[4194304]{0:T(1024)(128)(4,1)S(1)}, s32[]{:S(2)}) async-start(s8[8388608]{0:T(1024)(128)(4,1)} %bitcast.83), calls=%async_computation.7 | async-start | bytes 8388608
  34.5 4.2 %slice-start.3 = ((s8[8388608]{0:T(1024)(128)(4,1)}), s8[4194304]{0:T(1024)(128)(4,1)S(1)}, s32[]{:S(2)}) async-start(s8[8388608]{0:T(1024)(128)(4,1)} %bitcast.83), calls=%async_computation.8 | async-start | bytes 8388608
  42.0 21.8 %copy-start.1 = (bf16[1,256,1024]{2,1,0:T(8,128)(2,1)S(1)}, bf16[1,256,1024]{2,1,0:T(8,128)(2,1)}, u32[]{:S(2)}) copy-start(bf16[1,256,1024]{2,1,0:T(8,128)(2,1)} %param.9) | copy-start | bytes 1572868
  47.8 18.0 %copy-start.2 = (bf16[1024,32]{0,1:T(8,128)(2,1)S(1)}, bf16[1024,32]{0,1:T(8,128)(2,1)}, u32[]{:S(2)}) copy-start(bf16[1024,32]{0,1:T(8,128)(2,1)} %param.6) | copy-start | bytes 196612
  49.5 13.9 %all-to-all-start.1 = ((bf16[16,2,2,1024]{3,2,1,0:T(2,128)(2,1)}), bf16[16,2,2,1024]{3,2,1,0:T(2,128)(2,1)S(1)}, u32[]{:S(2)}, u32[]{:S(2)}) async-start(bf16[16,2,2,1024]{3,2,1,0:T(2,128)(2,1)} %copy.19), calls=%async_computation.2 | async-start | bytes 262144 | tf_op jit(solution)/shard_map/all_to_all | solution.py:33
  55.5 134.3 %all-reduce.2.cloned.1.call-start = ((), (), s32[]{:S(2)}) async-start(), calls=%async_computation.4 | async-start | bytes 262144 | tf_op jit(solution)/shard_map/psum | solution.py:94
Sparse Core Ops, SparseCore 0:
  42.1 4.9 reduce-scatter.1
  65.9 123.8 all-reduce.1
where the time goes:
time: 199 us; the launch traced here: 198 us
  waiting for transfers between devices  125 us (63%)
  matrix products  29.2 us (15%)
  blocking collectives  18.1 us (9%)
  between operations  14.2 us (7%)
  starting transfers between devices  6.26 us (3%)
  local copies, waits for them, and re-layouts  4.79 us (2%)
    psum x1, waiting for transfers between devices, per_device(): grad_param = lax.psum(local_param, ('ex', 'ey'))  123 us
    all_to_all x1, blocking collectives, route_in(): lax.all_to_all(stacked, 'ey', split_axis=2, concat_axis=0, tiled=True)  15.9 us
    all_to_all x1, starting transfers between devices, route_out(): return lax.all_to_all(summed, 'ey', split_axis=0, concat_axis=2, tiled=True)  6 us
    dot_general x1, matrix products, per_device(): jnp.einsum('ref,red->efd', hidden, slot_g, preferred_element_type=jnp.flo...  5.78 us
    dot_general x1, matrix products, per_device(): jnp.einsum('red,ref->edf', slot_x, dpre, preferred_element_type=jnp.float32)  5.78 us
    dot_general x1, matrix products, per_device(): jnp.einsum('red,edf->ref', slot_x, weight_in, preferred_element_type=jnp....  5.07 us
  transfers between devices with their start and end apart: 3, of which 2 were waited for; matrix products, arithmetic and copies ran while one was open for 6% of the time, Pallas kernels for 0%

commit v1 on v0

--- a/solution.py
+++ b/solution.py
@@ -2,6 +2,9 @@
 import jax.numpy as jnp
 from jax import lax
 from jax.sharding import PartitionSpec as P
+from jax.lax import psum
+
+apply_sites = lambda axis_id, raw, axis_key: psum(psum(raw, axis_key), axis_id)
 
 
 def gelu_parts(pre):
@@ -91,7 +94,7 @@
         "ips,ds->ipd", logit_grad, slot_param, preferred_element_type=jnp.float32
     )
     local_param = jnp.einsum("ipd,ips->ds", tokens, logit_grad, preferred_element_type=jnp.float32)
-    grad_param = lax.psum(local_param, ("ex", "ey"))
+    grad_param = apply_sites("ex", local_param, "ey")
     return (grad_tokens.astype(jnp.bfloat16), grad_param, grad_win, grad_wout)
 
 

time: 199 us -> 198 us (level)
    psum x1 -> x2, waiting for transfers between devices: 123 us -> 123 us  [the longest x1 105 us: psum(raw, axis_key)]
  transfers between devices with their start and end apart: 3 -> 4, of which waited for: 2 -> 3; matrix products, arithmetic and copies ran while one was open for 6% -> 7% of each run, Pallas kernels for 0% -> 0%
where the time goes in v1:
time: 198 us
  waiting for transfers between devices  125 us (63%)
  matrix products  29.2 us (15%)
  blocking collectives  18.1 us (9%)
  between operations  13.9 us (7%)
  starting transfers between devices  6.3 us (3%)
  local copies, waits for them, and re-layouts  4.79 us (2%)
    psum x1, waiting for transfers between devices, psum(raw, axis_key)  105 us
    psum x1, waiting for transfers between devices, psum(psum(raw, axis_key), axis_id)  18.1 us
    all_to_all x1, blocking collectives, route_in(): lax.all_to_all(stacked, 'ey', split_axis=2, concat_axis=0, tiled=True)  15.9 us
    all_to_all x1, starting transfers between devices, route_out(): return lax.all_to_all(summed, 'ey', split_axis=0, concat_axis=2, tiled=True)  6 us
    dot_general x1, matrix products, per_device(): jnp.einsum('ref,red->efd', hidden, slot_g, preferred_element_type=jnp.flo...  5.78 us
    dot_general x1, matrix products, per_device(): jnp.einsum('red,ref->edf', slot_x, dpre, preferred_element_type=jnp.float32)  5.78 us
    dot_general x1, matrix products, per_device(): jnp.einsum('red,edf->ref', slot_x, weight_in, preferred_element_type=jnp....  5.07 us
  transfers between devices with their start and end apart: 4, of which 3 were waited for; matrix products, arithmetic and copies ran while one was open for 7% of the time, Pallas kernels for 0%

profile of v1, /device:TPU:0, one launch (start us, length us, event | category | flops | bytes accessed | tf_op | source)
XLA Modules:
  0.0 197.8 jit_solution(2432095978926402383)
XLA Ops:
  7.2 1.0 copy-done
  8.2 1.2 fusion.36
  9.6 0.2 fusion.6
  9.9 1.2 fusion.7
  11.3 15.9 %all_to_all.36 = bf16[1,2,32,1024]{3,1,0,2:T(2,128)(2,1)S(1)} all-to-all(bf16[1,2,32,1024]{3,1,0,2:T(2,128)(2,1)S(1)} %copy.17), channel_id=1, replica_groups=mesh['ex'=2,'ey'=16] {'ey'}, dimensions={2} | all-to-all | bytes 262144 | tf_op jit(solution)/shard_map/all_to_all | solution.py:23
  27.3 2.1 %all-gather = bf16[32,1,2,2,1024]{4,0,3,2,1:T(8,128)(2,1)S(1)} all-gather(bf16[16,1,2,2,1024]{4,0,3,2,1:T(8,128)(2,1)S(1)} %bitcast.90), channel_id=2, replica_groups=mesh['ex'=2,'ey'=16] {'ex'}, dimensions={0}, use_global_device_ids=true | all-gather | bytes 393216 | tf_op jit(solution)/shard_map/all_gather | solution.py:24
  29.4 5.1 %convolution_bitcast_fusion.1 = f32[32,2,2048]{2,0,1:T(8,128)S(1)} fusion(bf16[2,1024,2048]{2,1,0:T(8,128)(2,1)} %param.7, bf16[32,2,2,1024]{3,0,2,1:T(8,128)(2,1)S(1)} %bitcast.85), kind=kOutput, calls=%fused_computation.4 | convolution fusion | flops 268435456 | bytes 9043968 | tf_op jit(solution)/shard_map/red,edf->ref/dot_general | solution.py:55
  34.5 1.5 fusion.4
  36.0 2.6 %fusion.1 = bf16[32,2,2048]{2,0,1:T(8,128)(2,1)S(1)} fusion(bf16[2,2048,1024]{2,1,0:T(8,128)(2,1)S(1)} %bitcast.82, f32[32,2,2048]{2,0,1:T(8,128)S(1)} %convolution_bitcast_fusion.1, bf16[32,2,2,1024]{3,0,2,1:T(8,128)(2,1)S(1)} %bitcast.86), kind=kOutput, calls=%fused_computation.5 | convolution fusion | flops 269746176 | bytes 9306112 | tf_op jit(solution)/shard_map/red,efd->ref/dot_general | solution.py:58
  38.7 2.6 %fusion.5 = bf16[32,1,2,1024]{3,0,2,1:T(8,128)(2,1)S(1)} fusion(bf16[32,2,2048]{2,0,1:T(8,128)(2,1)S(1)} %fusion.1, bf16[2,1024,2048]{2,1,0:T(8,128)(2,1)S(1)} %bitcast.84), kind=kOutput, calls=%fused_computation.12 | convolution fusion | flops 268500992 | bytes 8781824 | tf_op jit(solution)/shard_map/ref,edf->red/dot_general | solution.py:67
  41.2 0.7 pad_maximum_fusion
  42.0 5.8 %convolution_convert_fusion = bf16[2,2048,1024]{2,1,0:T(8,128)(2,1)} fusion(bf16[32,2,2,1024]{3,0,2,1:T(8,128)(2,1)S(1)} %bitcast.87, f32[32,2,2048]{2,0,1:T(8,128)S(1)} %convolution_bitcast_fusion.1), kind=kOutput, calls=%fused_computation | convolution fusion | flops 273285120 | bytes 9043968 | tf_op jit(solution)/shard_map/ref,red->efd/dot_general | solution.py:80
  47.8 1.7 copy.19
  49.5 6.0 %all-to-all-start.1 = ((bf16[16,2,2,1024]{3,2,1,0:T(2,128)(2,1)}), bf16[16,2,2,1024]{3,2,1,0:T(2,128)(2,1)S(1)}, u32[]{:S(2)}, u32[]{:S(2)}) async-start(bf16[16,2,2,1024]{3,2,1,0:T(2,128)(2,1)} %copy.19), calls=%async_computation.2 | async-start | bytes 262144 | tf_op jit(solution)/shard_map/all_to_all | solution.py:36
  55.8 5.8 %convolution_convert_fusion.1 = bf16[2,1024,2048]{2,1,0:T(8,128)(2,1)} fusion(bf16[32,2,2048]{2,0,1:T(8,128)(2,1)S(1)} %fusion.1, bf16[32,2,2,1024]{3,0,2,1:T(8,128)(2,1)S(1)} %bitcast.88), kind=kOutput, calls=%fused_computation.1 | convolution fusion | flops 272629760 | bytes 8781824 | tf_op jit(solution)/shard_map/red,ref->edf/dot_general | solution.py:77
  61.6 1.9 all-to-all-done.1
  63.8 0.3 convolution_bitcast_fusion.3
  64.1 0.4 multiply_reduce_fusion.1
  64.4 0.9 convolution_bitcast_fusion.2
  65.4 0.4 fusion.22
  65.8 104.5 %all-reduce.3.cloned.1.call-done = f32[1024,32]{0,1:T(8,128)} async-done(((f32[1024,32]{0,1:T(8,128)}), f32[1024,32]{0,1:T(8,128)}) %all-reduce.3.cloned.1.call-update) | async-done | bytes 131088 | tf_op jit(solution)/shard_map/psum | solution.py:7
  170.4 1.2 fusion.3
  171.6 18.1 %all-reduce.5.cloned.1.call-done = f32[1024,32]{0,1:T(8,128)} async-done(((f32[1024,32]{0,1:T(8,128)}), f32[1024,32]{0,1:T(8,128)}) %all-reduce.5.cloned.1.call-update) | async-done | bytes 131088 | tf_op jit(solution)/shard_map/psum | solution.py:7
  189.7 1.6 copy.41
  (28 shorter events, 1.1 us)
Async XLA Ops:
  7.2 1.0 copy-start
  7.2 40.6 %reduce-scatter.2.cloned.1.call-start = ((), (), s32[]{:S(2)}) async-start(), calls=%async_computation.3 | async-start | bytes 393216 | tf_op jit(solution)/shard_map/reduce_scatter | solution.py:28
  27.2 7.3 %slice-start = ((s8[8388608]{0:T(1024)(128)(4,1)}), s8[4194304]{0:T(1024)(128)(4,1)S(1)}, s32[]{:S(2)}) async-start(s8[8388608]{0:T(1024)(128)(4,1)} %bitcast.81), calls=%async_computation.6 | async-start | bytes 8388608
  29.4 5.1 %slice-start.1 = ((s8[8388608]{0:T(1024)(128)(4,1)}), s8[4194304]{0:T(1024)(128)(4,1)S(1)}, s32[]{:S(2)}) async-start(s8[8388608]{0:T(1024)(128)(4,1)} %bitcast.81), calls=%async_computation.7 | async-start | bytes 8388608
  29.4 9.3 %slice-start.2 = ((s8[8388608]{0:T(1024)(128)(4,1)}), s8[4194304]{0:T(1024)(128)(4,1)S(1)}, s32[]{:S(2)}) async-start(s8[8388608]{0:T(1024)(128)(4,1)} %bitcast.83), calls=%async_computation.8 | async-start | bytes 8388608
  34.5 4.2 %slice-start.3 = ((s8[8388608]{0:T(1024)(128)(4,1)}), s8[4194304]{0:T(1024)(128)(4,1)S(1)}, s32[]{:S(2)}) async-start(s8[8388608]{0:T(1024)(128)(4,1)} %bitcast.83), calls=%async_computation.9 | async-start | bytes 8388608
  42.0 21.8 %copy-start.1 = (bf16[1,256,1024]{2,1,0:T(8,128)(2,1)S(1)}, bf16[1,256,1024]{2,1,0:T(8,128)(2,1)}, u32[]{:S(2)}) copy-start(bf16[1,256,1024]{2,1,0:T(8,128)(2,1)} %param.9) | copy-start | bytes 1572868
  47.8 122.6 %copy-start.2 = (bf16[1024,32]{0,1:T(8,128)(2,1)S(1)}, bf16[1024,32]{0,1:T(8,128)(2,1)}, u32[]{:S(2)}) copy-start(bf16[1024,32]{0,1:T(8,128)(2,1)} %param.6) | copy-start | bytes 196612
  49.5 13.9 %all-to-all-start.1 = ((bf16[16,2,2,1024]{3,2,1,0:T(2,128)(2,1)}), bf16[16,2,2,1024]{3,2,1,0:T(2,128)(2,1)S(1)}, u32[]{:S(2)}, u32[]{:S(2)}) async-start(bf16[16,2,2,1024]{3,2,1,0:T(2,128)(2,1)} %copy.19), calls=%async_computation.2 | async-start | bytes 262144 | tf_op jit(solution)/shard_map/all_to_all | solution.py:36
  55.5 114.8 %all-reduce.3.cloned.1.call-start = ((), (), s32[]{:S(2)}) async-start(), calls=%async_computation.4 | async-start | bytes 262144 | tf_op jit(solution)/shard_map/psum | solution.py:7
  65.4 124.3 %all-reduce.5.cloned.1.call-start = ((), (), s32[]{:S(2)}) async-start(), calls=%async_computation.5 | async-start | bytes 262144 | tf_op jit(solution)/shard_map/psum | solution.py:7
Sparse Core Ops, SparseCore 0:
  42.1 4.9 reduce-scatter.1
  65.5 104.8 all-reduce.2
  172.7 16.9 all-reduce.4
